TPU v7x, 256 devices: a whole 4x4x8 slice. The times are simulated.
256 devices in a mesh: gx: 16 (over z, core), gy: 16 (over x, y).
Axes of the slice: x: 4, y: 4, z: 8, core: 2. Of those that a mesh axis runs over, the one named last changes fastest.
Arguments:
- features: bfloat16 [256, 256, 1, 1024], P('gx', 'gy'), may hold values from -6 to 6
- slot_map: int32 [16, 16, 2], replicated, may hold values from -1 to 0, as said below
- tap_weights: float32 [27, 64], replicated, may hold values from -1.25 to 1.25
- gain: float32 [64], replicated, may hold values from 0.5 to 1.5
- mix_weight: bfloat16 [64, 64], replicated, may hold values from -0.75 to 0.75
- cotangent: bfloat16 [256, 256, 1, 1024], P('gx', 'gy'), may hold values from -6 to 6
Outputs:
- mixed: bfloat16 [256, 256, 1, 1024], P('gx', 'gy')
- grad_features: bfloat16 [256, 256, 1, 1024], P('gx', 'gy')
- grad_taps: float32 [27, 64], replicated
- grad_gain: float32 [64], replicated
- grad_mix: float32 [64, 64], replicated
Inputs may be any that keep to these rules, and one draw needn't show every extreme that they name: `slot_map`: in each block column the active levels carry slot numbers 0, 1, 2, ... in increasing level order and the others carry -1; every block column has exactly 1 active block.
All inputs are finite; a program needn't handle non-finite values.
Results may differ from a plain program's by a relative error of at most 0.0039.
Values may be sent and summed in bfloat16 or wider, within the bound.
A program may use at most 128 MiB of HBM per device.

v0:
```python
import jax
import jax.numpy as jnp
from jax import lax
from jax.sharding import PartitionSpec as P

EPS = 1e-05


def extended_2(cells, sides, width):
    for axis, dim in sides:
        count = lax.axis_size(axis)
        ends = count - 1
        head = lax.slice_in_dim(cells, 0, width, axis=dim)
        tail = lax.slice_in_dim(cells, cells.shape[dim] - width, cells.shape[dim], axis=dim)
        cells = jnp.concatenate(
            [
                lax.ppermute(tail, axis, [(i, (i + 1) % count) for i in range(ends)]),
                cells,
                lax.ppermute(head, axis, [((i + 1) % count, i) for i in range(ends)]),
            ],
            axis=dim,
        )
    return cells


def one_hot_map(level_slots, slot_count):
    slot_ids = jnp.arange(slot_count, dtype=jnp.int32)
    return (level_slots[..., None] == slot_ids).astype(jnp.bfloat16)


def slot_lookup(center, slot_count):
    slot_ids = jnp.arange(slot_count, dtype=jnp.int32)
    matches = center[:, None] == slot_ids[None, :]
    level_ids = jnp.arange(center.shape[0], dtype=jnp.int32)[:, None]
    position = jnp.sum(jnp.where(matches, level_ids, 0), axis=0)
    active = jnp.any(matches, axis=0)
    return (position, active)


def slot_slabs(extended, position, active, channels):
    levels = extended.shape[2]
    level_pad = jnp.pad(extended, ((0, 0), (0, 0), (1, 1), (0, 0)))
    level_ids = jnp.arange(levels + 2, dtype=jnp.int32)
    wanted = position[:, None] + jnp.arange(3, dtype=jnp.int32)[None, :]
    select = (wanted[:, :, None] == level_ids[None, None, :]) & active[:, None, None]
    picked = jnp.einsum(
        "xypf,skp->xyskf",
        level_pad,
        select.astype(jnp.bfloat16),
        preferred_element_type=jnp.float32,
    ).astype(jnp.bfloat16)
    below = picked[:, :, :, 0, -channels:]
    middle = picked[:, :, :, 1, :]
    above = picked[:, :, :, 2, :channels]
    return jnp.concatenate([below, middle, above], axis=-1)


def stencil(padded, taps):
    channels = taps.shape[1]
    inner = padded.shape[0] - 2
    length = padded.shape[-1] - 2 * channels
    accum_sum = jnp.zeros((inner, inner) + padded.shape[2:-1] + (length,), jnp.float32)
    for tap_index in range(27):
        off_x = tap_index // 9
        off_y = tap_index // 3 % 3
        off_z = tap_index % 3
        shifted = padded[
            off_x : off_x + inner,
            off_y : off_y + inner,
            ...,
            channels * off_z : channels * off_z + length,
        ].astype(jnp.float32)
        accum_sum = accum_sum + shifted * jnp.tile(taps[tap_index], length // channels)
    return accum_sum


def tap_grads(padded, grads, channels):
    inner = padded.shape[0] - 2
    length = padded.shape[-1] - 2 * channels
    rows_out = []
    for tap_index in range(27):
        off_x = tap_index // 9
        off_y = tap_index // 3 % 3
        off_z = tap_index % 3
        shifted = padded[
            off_x : off_x + inner,
            off_y : off_y + inner,
            ...,
            channels * off_z : channels * off_z + length,
        ].astype(jnp.float32)
        rows_out.append(jnp.sum((shifted * grads).reshape(-1, channels), axis=0))
    return jnp.stack(rows_out)


def norm_forward(depth_slots):
    mean_square = jnp.mean(depth_slots * depth_slots, axis=-1, keepdims=True)
    inv_rms = lax.rsqrt(mean_square + EPS)
    return (depth_slots * inv_rms, inv_rms)


def norm_backward(grad_norm, normed, inv_rms, gain):
    grad_scaled = grad_norm * gain
    return inv_rms * (grad_scaled - normed * jnp.mean(grad_scaled * normed, axis=-1, keepdims=True))


def shards(features, slot_map, tap_weights, gain, mix_weight, cotangent):
    block_side = features.shape[0]
    slot_count = features.shape[2]
    lane_width = features.shape[3]
    channels = gain.shape[0]
    depth_cells = lane_width // channels
    levels = slot_map.shape[2]
    cell_shape = (block_side, block_side, slot_count, depth_cells, channels)
    grid_row = lax.axis_index("gx")
    grid_col = lax.axis_index("gy")
    padded_map = jnp.pad(slot_map, ((1, 1), (1, 1), (0, 0)), constant_values=-1)
    near_maps = lax.dynamic_slice(padded_map, (grid_row, grid_col, jnp.int32(0)), (3, 3, levels))
    center = near_maps[1, 1]
    position, active = slot_lookup(center, slot_count)
    keep_mask = active.astype(jnp.float32)[None, None, :, None, None]

    def extend(slot_data):
        dense_field = jnp.einsum(
            "xysf,ps->xypf",
            slot_data,
            one_hot_map(center, slot_count),
            preferred_element_type=jnp.float32,
        ).astype(jnp.bfloat16)
        extended = extended_2(dense_field, (("gx", 0), ("gy", 1)), 1)
        return slot_slabs(extended, position, active, channels)

    padded_in = extend(features)
    depth_slots = stencil(padded_in, tap_weights).reshape(cell_shape)
    normed, inv_rms = norm_forward(depth_slots)
    norm_bf = (normed * gain).astype(jnp.bfloat16)
    branch = jnp.einsum("xyszc,cd->xyszd", norm_bf, mix_weight, preferred_element_type=jnp.float32)
    mixed = (
        ((features.reshape(cell_shape).astype(jnp.float32) + branch) * keep_mask)
        .astype(jnp.bfloat16)
        .reshape(features.shape)
    )
    grad_out = cotangent.reshape(cell_shape) * keep_mask.astype(jnp.bfloat16)
    grad_mix_part = jnp.einsum(
        "xyszc,xyszd->cd", norm_bf, grad_out, preferred_element_type=jnp.float32
    )
    grad_norm = jnp.einsum(
        "xyszd,cd->xyszc", grad_out, mix_weight, preferred_element_type=jnp.float32
    )
    grad_gain_part = jnp.sum(grad_norm * normed, axis=(0, 1, 2, 3))
    grad_depth = (
        (norm_backward(grad_norm, normed, inv_rms, gain) * keep_mask)
        .astype(jnp.bfloat16)
        .reshape(features.shape)
    )
    padded_grad = extend(grad_depth)
    back_slots = stencil(padded_grad, tap_weights[::-1])
    grad_features = (
        ((cotangent.astype(jnp.float32) + back_slots).reshape(cell_shape) * keep_mask)
        .astype(jnp.bfloat16)
        .reshape(features.shape)
    )
    grad_center = padded_grad[1:-1, 1:-1, :, channels:-channels].astype(jnp.float32)
    grad_taps_part = tap_grads(padded_in, grad_center, channels)
    grad_taps, grad_mix, grad_gain = lax.psum(
        (grad_taps_part, grad_mix_part, grad_gain_part), ("gx", "gy")
    )
    return (mixed, grad_features, grad_taps, grad_gain, grad_mix)


def solution(mesh):
    return jax.shard_map(
        shards,
        mesh=mesh,
        in_specs=(P("gx", "gy", None, None), P(), P(), P(), P(), P("gx", "gy", None, None)),
        out_specs=(P("gx", "gy", None, None), P("gx", "gy", None, None), P(), P(), P()),
        check_vma=False,
    )
```

profile of v0, /device:TPU:1, one launch (start us, length us, event | category | flops | bytes accessed | tf_op | source)
XLA Modules:
  0.0 338.6 jit_solution(7447671005226463131)
XLA Ops:
  4.5 5.1 %collective-permute-start = (bf16[1,16,2,1024]{3,2,1,0:T(2,128)(2,1)S(1)}, bf16[1,16,2,1024]{3,2,1,0:T(2,128)(2,1)S(1)}, u32[]{:S(2)}, u32[]{:S(2)}) collective-permute-start(bf16[1,16,2,1024]{3,2,1,0:T(2,128)(2,1)S(1)} %get-tuple-element.75), channel_id=1, source_target_pairs={{0,16},{16,32},{32,48},{48,64},{64,80},{80,96},{96,112},{112,128},... | collective-permute-start | bytes 196616 | tf_op jit(solution)/shard_map/ppermute | solution.py:17
  19.4 3.2 collective-permute-start.2
  24.8 2.9 collective-permute-done.3
  27.8 4.5 %convert_bitcast_fusion.1 = bf16[18,18,1,3,1024]{4,3,1,0,2:T(4,128)(2,1)S(1)} fusion(bf16[18,1,2,1024]{3,2,1,0:T(2,128)(2,1)S(1)} %collective-permute-done.3, bf16[18,1,2,1024]{3,2,1,0:T(2,128)(2,1)S(1)} %collective-permute-done.2, bf16[1,16,2,1024]{3,2,1,0:T(2,128)(2,1)S(1)} %collective-permute-done.1, bf16[16,16,2,1024]{3,2,1,0:T(2,128)(2,1)S(1)} %fusion.52, ...), kind=kOutput, calls=%fused_computation.88 | convolution fusion | flops 32845848 | bytes 3317773 | tf_op jit(solution)/shard_map/xypf,skp->xyskf/dot_general | solution.py:46
  34.6 9.4 %fusion.125 = (f32[16,16,1,1024]{3,1,0,2:T(8,128)}, f32[16,16,1,1024]{3,1,0,2:T(8,128)}) fusion(f32[1024]{0:T(1024)S(1)} %mul.720, bf16[18,18,1,64]{3,1,0,2:T(8,128)(2,1)S(1)} %get-tuple-element.105, bf16[18,18,1,1024]{3,1,0,2:T(8,128)(2,1)S(1)} %bitcast.278, f32[1024]{0:T(1024)S(1)} %mul.717, f32[1024]{0:T(1024)S(1)} %mul.714, ...), kind=kLoop, calls=%fused_computation.308 | loop fusion | flops 35389440 | bytes 8032256 | tf_op jit(solution)/shard_map/mul | solution.py:96
  52.8 3.1 multiply_convert_fusion.2
  65.5 5.1 %collective-permute-start.4 = (bf16[1,16,2,1024]{3,2,1,0:T(2,128)(2,1)}, bf16[1,16,2,1024]{3,2,1,0:T(2,128)(2,1)}, u32[]{:S(2)}, u32[]{:S(2)}) collective-permute-start(bf16[1,16,2,1024]{3,2,1,0:T(2,128)(2,1)} %get-tuple-element.73), channel_id=1, source_target_pairs={{0,16},{16,32},{32,48},{48,64},{64,80},{80,96},{96,112},{112,128},... | collective-permute-start | bytes 196616 | tf_op jit(solution)/shard_map/ppermute | solution.py:17
  77.3 3.2 collective-permute-start.6
  83.5 3.0 reshape.456
  86.6 5.0 %convert_bitcast_fusion = bf16[18,18,1,3,1024]{4,3,1,0,2:T(4,128)(2,1)S(1)} fusion(bf16[18,1,2,1024]{3,2,1,0:T(2,128)(2,1)S(1)} %collective-permute-done.7, bf16[18,1,2,1024]{3,2,1,0:T(2,128)(2,1)S(1)} %collective-permute-done.6, bf16[1,16,2,1024]{3,2,1,0:T(2,128)(2,1)} %collective-permute-done.5, bf16[16,16,2,1024]{3,2,1,0:T(2,128)(2,1)S(1)} %fusion.54, ...), kind=kOutput, calls=%fused_computation.87 | convolution fusion | flops 32845848 | bytes 3317773 | tf_op jit(solution)/shard_map/xypf,skp->xyskf/dot_general | solution.py:46
  93.8 4.0 %convert_multiply_fusion.2 = (f32[16,16,1,1024]{3,1,0,2:T(8,128)}, f32[16,16,1,1024]{3,1,0,2:T(8,128)}, f32[16,16,1,1024]{3,1,0,2:T(8,128)}, f32[16,16,1,1024]{3...) fusion(bf16[18,18,1,1024]{3,1,0,2:T(8,128)(2,1)S(1)} %bitcast.279, ...), kind=kLoop, calls=%fused_computation.2 | loop fusion | flops 8126464 | bytes 7520768 | tf_op jit(solution)/shard_map/mul | solution.py:91
  97.7 4.4 %convert_multiply_fusion.3 = (f32[16,16,1,1024]{3,1,0,2:T(8,128)}, f32[16,16,1,1024]{3,1,0,2:T(8,128)}, f32[16,16,1,1024]{3,1,0,2:T(8,128)}, f32[16,16,1,1024]{3...) fusion(bf16[18,18,1,64]{3,1,0,2:T(8,128)(2,1)S(1)} %copy-done.10, ...), kind=kLoop, calls=%fused_computation.3 | loop fusion | flops 8126464 | bytes 7562240 | tf_op jit(solution)/shard_map/mul | solution.py:91
  102.2 4.3 %convert_multiply_fusion = (f32[16,16,1,1024]{3,1,0,2:T(8,128)}, f32[16,16,1,1024]{3,1,0,2:T(8,128)}, f32[16,16,1,1024]{3,1,0,2:T(8,128)}, f32[16,16,1,1024]{3,1...) fusion(bf16[18,18,1,64]{3,1,0,2:T(8,128)(2,1)S(1)} %copy-done.10, ...), kind=kLoop, calls=%fused_computation | loop fusion | flops 8126464 | bytes 7520768 | tf_op jit(solution)/shard_map/mul | solution.py:91
  106.4 4.0 %convert_multiply_fusion.1 = (f32[16,16,1,1024]{3,1,0,2:T(8,128)}, f32[16,16,1,1024]{3,1,0,2:T(8,128)}, f32[16,16,1,1024]{3,1,0,2:T(8,128)}, f32[16,16,1,1024]{3...) fusion(bf16[18,18,1,1024]{3,1,0,2:T(8,128)(2,1)S(1)} %bitcast.2, ...), kind=kLoop, calls=%fused_computation.1 | loop fusion | flops 4980736 | bytes 14680064 | tf_op jit(solution)/shard_map/mul | solution.py:91
  110.4 2.9 reshape.482
  115.4 2.8 reshape.458
  120.4 3.0 reshape.461
  125.6 2.8 reshape.464
  130.6 2.8 reshape.467
  135.6 2.8 reshape.470
  140.6 2.8 reshape.481
  185.5 3.1 reshape.466
  245.2 9.3 %fusion.106 = bf16[16,16,1,1024]{3,1,2,0:T(8,128)(2,1)} fusion(f32[]{:T(128)S(6)} %convert_element_type.307, f32[1024]{0:T(1024)S(1)} %copy-done.14, bf16[18,18,1,64]{3,1,0,2:T(8,128)(2,1)S(1)} %bitcast.290, bf16[18,18,1,1024]{3,1,0,2:T(8,128)(2,1)S(1)} %bitcast.287, f32[1024]{0:T(1024)S(1)} %mul.645, f32[1024]{0:T(1024)S(1)} %mul.648, ...), kind=kLoop, calls=%fused_computation.245 | loop fusion | flops 36175872 | bytes 6983684
  254.5 83.8 %all-reduce.3 = (f32[27,64]{1,0:T(8,128)}, f32[64]{0:T(128)}, f32[64,64]{1,0:T(8,128)}) all-reduce(f32[27,64]{1,0:T(8,128)S(1)} %stack.111, f32[64]{0:T(128)S(1)} %copy-done.54, f32[64,64]{1,0:T(8,128)S(1)} %convolution_bitcast_fusion), channel_id=1, replica_groups=mesh['gx'=16,'gy'=16] {'gx','gy'}, use_global_device_ids=true, to_apply=%region_31.32 | all-reduce | flops 5888 | bytes 47104 | tf_op jit(solution)/shard_map/psum | solution.py:164
  (266 shorter events, 158.7 us)
Async XLA Ops:
  0.6 52.2 %copy-start = (bf16[64,64]{1,0:T(8,128)(2,1)S(1)}, bf16[64,64]{1,0:T(8,128)(2,1)}, u32[]{:S(2)}) copy-start(bf16[64,64]{1,0:T(8,128)(2,1)} %param.10) | copy-start | bytes 24580
  4.5 14.7 %collective-permute-start = (bf16[1,16,2,1024]{3,2,1,0:T(2,128)(2,1)S(1)}, bf16[1,16,2,1024]{3,2,1,0:T(2,128)(2,1)S(1)}, u32[]{:S(2)}, u32[]{:S(2)}) collective-permute-start(bf16[1,16,2,1024]{3,2,1,0:T(2,128)(2,1)S(1)} %get-tuple-element.75), channel_id=1, source_target_pairs={{0,16},{16,32},{32,48},{48,64},{64,80},{80,96},{96,112},{112,128},... | collective-permute-start | bytes 196616 | tf_op jit(solution)/shard_map/ppermute | solution.py:17
  9.6 9.6 %collective-permute-start.1 = (bf16[1,16,2,1024]{3,2,1,0:T(2,128)(2,1)S(1)}, bf16[1,16,2,1024]{3,2,1,0:T(2,128)(2,1)S(1)}, u32[]{:S(2)}, u32[]{:S(2)}) collective-permute-start(bf16[1,16,2,1024]{3,2,1,0:T(2,128)(2,1)S(1)} %get-tuple-element.76), channel_id=1, source_target_pairs={{16,0},{32,16},{48,32},{64,48},{80,64},{96,80},{112,96},{128,112},... | collective-permute-start | bytes 196616 | tf_op jit(solution)/shard_map/ppermute | solution.py:19
  15.5 18.9 %copy-start.13 = (f32[1024]{0:T(1024)}, f32[1024]{0:T(1024)S(1)}, u32[]{:S(2)}) copy-start(f32[1024]{0:T(1024)S(1)} %mul.642) | copy-start | bytes 12292
  15.6 18.9 %copy-start.15 = (f32[1024]{0:T(1024)}, f32[1024]{0:T(1024)S(1)}, u32[]{:S(2)}) copy-start(f32[1024]{0:T(1024)S(1)} %mul.714) | copy-start | bytes 12292
  15.7 18.8 %copy-start.17 = (f32[1024]{0:T(1024)}, f32[1024]{0:T(1024)S(1)}, u32[]{:S(2)}) copy-start(f32[1024]{0:T(1024)S(1)} %mul.711) | copy-start | bytes 12292
  15.7 18.7 %copy-start.19 = (f32[1024]{0:T(1024)}, f32[1024]{0:T(1024)S(1)}, u32[]{:S(2)}) copy-start(f32[1024]{0:T(1024)S(1)} %mul.708) | copy-start | bytes 12292
  15.8 18.7 %copy-start.21 = (f32[1024]{0:T(1024)}, f32[1024]{0:T(1024)S(1)}, u32[]{:S(2)}) copy-start(f32[1024]{0:T(1024)S(1)} %mul.705) | copy-start | bytes 12292
  15.9 18.6 %copy-start.23 = (f32[1024]{0:T(1024)}, f32[1024]{0:T(1024)S(1)}, u32[]{:S(2)}) copy-start(f32[1024]{0:T(1024)S(1)} %mul.702) | copy-start | bytes 12292
  16.0 18.5 %copy-start.25 = (f32[1024]{0:T(1024)}, f32[1024]{0:T(1024)S(1)}, u32[]{:S(2)}) copy-start(f32[1024]{0:T(1024)S(1)} %mul.699) | copy-start | bytes 12292
  16.0 18.5 %copy-start.27 = (f32[1024]{0:T(1024)}, f32[1024]{0:T(1024)S(1)}, u32[]{:S(2)}) copy-start(f32[1024]{0:T(1024)S(1)} %mul.696) | copy-start | bytes 12292
  16.1 18.4 %copy-start.29 = (f32[1024]{0:T(1024)}, f32[1024]{0:T(1024)S(1)}, u32[]{:S(2)}) copy-start(f32[1024]{0:T(1024)S(1)} %mul.693) | copy-start | bytes 12292
  16.2 18.3 %copy-start.31 = (f32[1024]{0:T(1024)}, f32[1024]{0:T(1024)S(1)}, u32[]{:S(2)}) copy-start(f32[1024]{0:T(1024)S(1)} %mul.690) | copy-start | bytes 12292
  16.3 18.3 %copy-start.33 = (f32[1024]{0:T(1024)}, f32[1024]{0:T(1024)S(1)}, u32[]{:S(2)}) copy-start(f32[1024]{0:T(1024)S(1)} %mul.687) | copy-start | bytes 12292
  16.4 18.2 %copy-start.35 = (f32[1024]{0:T(1024)}, f32[1024]{0:T(1024)S(1)}, u32[]{:S(2)}) copy-start(f32[1024]{0:T(1024)S(1)} %mul.684) | copy-start | bytes 12292
  16.4 18.1 %copy-start.37 = (f32[1024]{0:T(1024)}, f32[1024]{0:T(1024)S(1)}, u32[]{:S(2)}) copy-start(f32[1024]{0:T(1024)S(1)} %mul.681) | copy-start | bytes 12292
  16.5 18.1 %copy-start.39 = (f32[1024]{0:T(1024)}, f32[1024]{0:T(1024)S(1)}, u32[]{:S(2)}) copy-start(f32[1024]{0:T(1024)S(1)} %mul.678) | copy-start | bytes 12292
  19.4 5.4 %collective-permute-start.2 = (bf16[18,1,2,1024]{3,2,1,0:T(2,128)(2,1)S(1)}, bf16[18,1,2,1024]{3,2,1,0:T(2,128)(2,1)S(1)}, u32[]{:S(2)}, u32[]{:S(2)}) collective-permute-start(bf16[18,1,2,1024]{3,2,1,0:T(2,128)(2,1)S(1)} %get-tuple-element.71), channel_id=1, source_target_pairs={{0,1},{1,2},{2,3},{3,4},{4,5},{5,6},{6,7},{7,8},{8,9},{9,10},{10,1... | collective-permute-start | bytes 221192 | tf_op jit(solution)/shard_map/ppermute | solution.py:17
  22.7 5.1 %collective-permute-start.3 = (bf16[18,1,2,1024]{3,2,1,0:T(2,128)(2,1)S(1)}, bf16[18,1,2,1024]{3,2,1,0:T(2,128)(2,1)S(1)}, u32[]{:S(2)}, u32[]{:S(2)}) collective-permute-start(bf16[18,1,2,1024]{3,2,1,0:T(2,128)(2,1)S(1)} %get-tuple-element.72), channel_id=1, source_target_pairs={{1,0},{2,1},{3,2},{4,3},{5,4},{6,5},{7,6},{8,7},{9,8},{10,9},{11,1... | collective-permute-start | bytes 221192 | tf_op jit(solution)/shard_map/ppermute | solution.py:19
  65.5 8.9 %collective-permute-start.4 = (bf16[1,16,2,1024]{3,2,1,0:T(2,128)(2,1)}, bf16[1,16,2,1024]{3,2,1,0:T(2,128)(2,1)}, u32[]{:S(2)}, u32[]{:S(2)}) collective-permute-start(bf16[1,16,2,1024]{3,2,1,0:T(2,128)(2,1)} %get-tuple-element.73), channel_id=1, source_target_pairs={{0,16},{16,32},{32,48},{48,64},{64,80},{80,96},{96,112},{112,128},... | collective-permute-start | bytes 196616 | tf_op jit(solution)/shard_map/ppermute | solution.py:17
  70.5 5.9 %collective-permute-start.5 = (bf16[1,16,2,1024]{3,2,1,0:T(2,128)(2,1)}, bf16[1,16,2,1024]{3,2,1,0:T(2,128)(2,1)}, u32[]{:S(2)}, u32[]{:S(2)}) collective-permute-start(bf16[1,16,2,1024]{3,2,1,0:T(2,128)(2,1)} %get-tuple-element.74), channel_id=1, source_target_pairs={{16,0},{32,16},{48,32},{64,48},{80,64},{96,80},{112,96},{128,112},... | collective-permute-start | bytes 196616 | tf_op jit(solution)/shard_map/ppermute | solution.py:19
  77.3 9.2 %collective-permute-start.6 = (bf16[18,1,2,1024]{3,2,1,0:T(2,128)(2,1)S(1)}, bf16[18,1,2,1024]{3,2,1,0:T(2,128)(2,1)S(1)}, u32[]{:S(2)}, u32[]{:S(2)}) collective-permute-start(bf16[18,1,2,1024]{3,2,1,0:T(2,128)(2,1)S(1)} %get-tuple-element.69), channel_id=1, source_target_pairs={{0,1},{1,2},{2,3},{3,4},{4,5},{5,6},{6,7},{7,8},{8,9},{9,10},{10,1... | collective-permute-start | bytes 221192 | tf_op jit(solution)/shard_map/ppermute | solution.py:17
  80.6 6.0 %collective-permute-start.7 = (bf16[18,1,2,1024]{3,2,1,0:T(2,128)(2,1)S(1)}, bf16[18,1,2,1024]{3,2,1,0:T(2,128)(2,1)S(1)}, u32[]{:S(2)}, u32[]{:S(2)}) collective-permute-start(bf16[18,1,2,1024]{3,2,1,0:T(2,128)(2,1)S(1)} %get-tuple-element.70), channel_id=1, source_target_pairs={{1,0},{2,1},{3,2},{4,3},{5,4},{6,5},{7,6},{8,7},{9,8},{10,9},{11,1... | collective-permute-start | bytes 221192 | tf_op jit(solution)/shard_map/ppermute | solution.py:19
  244.9 93.4 %copy-start.1 = (bf16[64,64]{1,0:T(8,128)(2,1)S(1)}, bf16[64,64]{1,0:T(8,128)(2,1)}, u32[]{:S(2)}) copy-start(bf16[64,64]{1,0:T(8,128)(2,1)} %param.10) | copy-start | bytes 24580
  (41 other events, 315.8 us)
where the time goes:
time: 344 us; the launch traced here: 339 us
  other arithmetic  105 us (31%)
  local copies, waits for them, and re-layouts  104 us (30%)
  blocking collectives  83.8 us (24%)
  starting transfers between devices  23.1 us (7%)
  matrix products  15.7 us (5%)
  waiting for transfers between devices  5.02 us (1%)
    psum x1, blocking collectives, shards(): lax.psum((grad_taps_part, grad_mix_part, grad_gain_part), ('gx', 'gy'))  83.8 us
    reshape x27, local copies, waits for them, and re-layouts, tap_grads(): rows_out.append(jnp.sum((shifted * grads).reshape(-1, channels), axis=0))  76.3 us
    reduce_sum x27, other arithmetic, tap_grads(): rows_out.append(jnp.sum((shifted * grads).reshape(-1, channels), axis=0))  57.9 us
    mul x4, other arithmetic, tap_grads(): rows_out.append(jnp.sum((shifted * grads).reshape(-1, channels), axis=0))  16.6 us
    ppermute x4, starting transfers between devices, extended_2(): lax.ppermute(tail, axis, [(i, (i + 1) % count) for i in range(ends)])  16.5 us
    dot_general x2, matrix products, slot_slabs(): jnp.einsum('xypf,skp->xyskf', level_pad, select.astype(jnp.bfloat16), pre...  9.5 us
    mul x1, other arithmetic, norm_forward(): mean_square = jnp.mean(depth_slots * depth_slots, axis=-1, keepdims=True)  9.4 us
    unnamed x1, other arithmetic  9.25 us
  transfers between devices with their start and end apart: 8, of which 2 were waited for; matrix products, arithmetic and copies ran while one was open for 4% of the time, Pallas kernels for 0%

commit v1 on v0

--- a/solution.py
+++ b/solution.py
@@ -162,7 +162,7 @@
     grad_center = padded_grad[1:-1, 1:-1, :, channels:-channels].astype(jnp.float32)
     grad_taps_part = tap_grads(padded_in, grad_center, channels)
     grad_taps, grad_mix, grad_gain = lax.psum(
-        (grad_taps_part, grad_mix_part, grad_gain_part), ("gx", "gy")
+        lax.psum((grad_taps_part, grad_mix_part, grad_gain_part), "gx"), "gy"
     )
     return (mixed, grad_features, grad_taps, grad_gain, grad_mix)
 

time: 344 us -> 383 us (1.11)
  the two profiles are of different devices: /device:TPU:1 before, /device:TPU:128 now
where the time goes in v1:
time: 383 us; the launch traced here: 378 us
  blocking collectives  123 us (32%)
  other arithmetic  105 us (27%)
  local copies, waits for them, and re-layouts  104 us (27%)
  starting transfers between devices  23.4 us (6%)
  matrix products  15.7 us (4%)
  waiting for transfers between devices  4.64 us (1%)
    reshape x27, local copies, waits for them, and re-layouts, tap_grads(): rows_out.append(jnp.sum((shifted * grads).reshape(-1, channels), axis=0))  76.3 us
    psum x1, blocking collectives, shards(): lax.psum(lax.psum((grad_taps_part, grad_mix_part, grad_gain_part), 'gx'),...  74.8 us
    reduce_sum x27, other arithmetic, tap_grads(): rows_out.append(jnp.sum((shifted * grads).reshape(-1, channels), axis=0))  57.9 us
    psum x1, blocking collectives, shards(): lax.psum((grad_taps_part, grad_mix_part, grad_gain_part), 'gx')  48.1 us
    mul x4, other arithmetic, tap_grads(): rows_out.append(jnp.sum((shifted * grads).reshape(-1, channels), axis=0))  16.6 us
    ppermute x4, starting transfers between devices, extended_2(): lax.ppermute(head, axis, [((i + 1) % count, i) for i in range(ends)])  12.5 us
    ppermute x4, starting transfers between devices, extended_2(): lax.ppermute(tail, axis, [(i, (i + 1) % count) for i in range(ends)])  10.9 us
    dot_general x2, matrix products, slot_slabs(): jnp.einsum('xypf,skp->xyskf', level_pad, select.astype(jnp.bfloat16), pre...  9.5 us
  transfers between devices with their start and end apart: 8, of which 3 were waited for; matrix products, arithmetic and copies ran while one was open for 4% of the time, Pallas kernels for 0%

profile of v1, /device:TPU:128, one launch (start us, length us, event | category | flops | bytes accessed | tf_op | source)
XLA Modules:
  0.0 377.6 jit_solution(2375702078115320836)
XLA Ops:
  6.6 4.9 %collective-permute-start.1 = (bf16[1,16,2,1024]{3,2,1,0:T(2,128)(2,1)S(1)}, bf16[1,16,2,1024]{3,2,1,0:T(2,128)(2,1)S(1)}, u32[]{:S(2)}, u32[]{:S(2)}) collective-permute-start(bf16[1,16,2,1024]{3,2,1,0:T(2,128)(2,1)S(1)} %get-tuple-element.79), channel_id=1, source_target_pairs={{16,0},{32,16},{48,32},{64,48},{80,64},{96,80},{112,96},{128,112},... | collective-permute-start | bytes 196616 | tf_op jit(solution)/shard_map/ppermute | solution.py:19
  19.4 3.5 collective-permute-start.2
  25.0 4.1 %collective-permute-done.3 = bf16[18,1,2,1024]{3,2,1,0:T(2,128)(2,1)S(1)} collective-permute-done((bf16[18,1,2,1024]{3,2,1,0:T(2,128)(2,1)S(1)}, bf16[18,1,2,1024]{3,2,1,0:T(2,128)(2,1)S(1)}, u32[]{:S(2)}, u32[]{:S(2)}) %collective-permute-start.3) | collective-permute-done | bytes 73760 | tf_op jit(solution)/shard_map/ppermute | solution.py:19
  29.1 4.5 %convert_bitcast_fusion.1 = bf16[18,18,1,3,1024]{4,3,1,0,2:T(4,128)(2,1)S(1)} fusion(bf16[18,1,2,1024]{3,2,1,0:T(2,128)(2,1)S(1)} %collective-permute-done.3, bf16[18,1,2,1024]{3,2,1,0:T(2,128)(2,1)S(1)} %collective-permute-done.2, bf16[1,16,2,1024]{3,2,1,0:T(2,128)(2,1)S(1)} %collective-permute-done.1, bf16[16,16,2,1024]{3,2,1,0:T(2,128)(2,1)S(1)} %fusion.52, ...), kind=kOutput, calls=%fused_computation.88 | convolution fusion | flops 32845848 | bytes 3317773 | tf_op jit(solution)/shard_map/xypf,skp->xyskf/dot_general | solution.py:46
  36.0 9.4 %fusion.125 = (f32[16,16,1,1024]{3,1,0,2:T(8,128)}, f32[16,16,1,1024]{3,1,0,2:T(8,128)}) fusion(f32[1024]{0:T(1024)S(1)} %mul.720, bf16[18,18,1,64]{3,1,0,2:T(8,128)(2,1)S(1)} %get-tuple-element.108, bf16[18,18,1,1024]{3,1,0,2:T(8,128)(2,1)S(1)} %bitcast.278, f32[1024]{0:T(1024)S(1)} %mul.717, f32[1024]{0:T(1024)S(1)} %mul.714, ...), kind=kLoop, calls=%fused_computation.308 | loop fusion | flops 35389440 | bytes 8032256 | tf_op jit(solution)/shard_map/mul | solution.py:96
  54.1 3.1 multiply_convert_fusion.2
  68.7 4.9 %collective-permute-start.5 = (bf16[1,16,2,1024]{3,2,1,0:T(2,128)(2,1)}, bf16[1,16,2,1024]{3,2,1,0:T(2,128)(2,1)}, u32[]{:S(2)}, u32[]{:S(2)}) collective-permute-start(bf16[1,16,2,1024]{3,2,1,0:T(2,128)(2,1)} %get-tuple-element.77), channel_id=1, source_target_pairs={{16,0},{32,16},{48,32},{64,48},{80,64},{96,80},{112,96},{128,112},... | collective-permute-start | bytes 196616 | tf_op jit(solution)/shard_map/ppermute | solution.py:19
  76.7 3.5 collective-permute-start.6
  83.2 3.0 reshape.456
  86.4 5.0 %convert_bitcast_fusion = bf16[18,18,1,3,1024]{4,3,1,0,2:T(4,128)(2,1)S(1)} fusion(bf16[18,1,2,1024]{3,2,1,0:T(2,128)(2,1)S(1)} %collective-permute-done.7, bf16[18,1,2,1024]{3,2,1,0:T(2,128)(2,1)S(1)} %collective-permute-done.6, bf16[1,16,2,1024]{3,2,1,0:T(2,128)(2,1)} %collective-permute-done.5, bf16[16,16,2,1024]{3,2,1,0:T(2,128)(2,1)S(1)} %fusion.54, ...), kind=kOutput, calls=%fused_computation.87 | convolution fusion | flops 32845848 | bytes 3317773 | tf_op jit(solution)/shard_map/xypf,skp->xyskf/dot_general | solution.py:46
  93.6 4.0 %convert_multiply_fusion.2 = (f32[16,16,1,1024]{3,1,0,2:T(8,128)}, f32[16,16,1,1024]{3,1,0,2:T(8,128)}, f32[16,16,1,1024]{3,1,0,2:T(8,128)}, f32[16,16,1,1024]{3...) fusion(bf16[18,18,1,1024]{3,1,0,2:T(8,128)(2,1)S(1)} %bitcast.279, ...), kind=kLoop, calls=%fused_computation.2 | loop fusion | flops 8126464 | bytes 7520768 | tf_op jit(solution)/shard_map/mul | solution.py:91
  97.6 4.4 %convert_multiply_fusion.3 = (f32[16,16,1,1024]{3,1,0,2:T(8,128)}, f32[16,16,1,1024]{3,1,0,2:T(8,128)}, f32[16,16,1,1024]{3,1,0,2:T(8,128)}, f32[16,16,1,1024]{3...) fusion(bf16[18,18,1,64]{3,1,0,2:T(8,128)(2,1)S(1)} %copy-done.10, ...), kind=kLoop, calls=%fused_computation.3 | loop fusion | flops 8126464 | bytes 7562240 | tf_op jit(solution)/shard_map/mul | solution.py:91
  102.0 4.3 %convert_multiply_fusion = (f32[16,16,1,1024]{3,1,0,2:T(8,128)}, f32[16,16,1,1024]{3,1,0,2:T(8,128)}, f32[16,16,1,1024]{3,1,0,2:T(8,128)}, f32[16,16,1,1024]{3,1...) fusion(bf16[18,18,1,64]{3,1,0,2:T(8,128)(2,1)S(1)} %copy-done.10, ...), kind=kLoop, calls=%fused_computation | loop fusion | flops 8126464 | bytes 7520768 | tf_op jit(solution)/shard_map/mul | solution.py:91
  106.3 4.0 %convert_multiply_fusion.1 = (f32[16,16,1,1024]{3,1,0,2:T(8,128)}, f32[16,16,1,1024]{3,1,0,2:T(8,128)}, f32[16,16,1,1024]{3,1,0,2:T(8,128)}, f32[16,16,1,1024]{3...) fusion(bf16[18,18,1,1024]{3,1,0,2:T(8,128)(2,1)S(1)} %bitcast.2, ...), kind=kLoop, calls=%fused_computation.1 | loop fusion | flops 4980736 | bytes 14680064 | tf_op jit(solution)/shard_map/mul | solution.py:91
  110.3 2.9 reshape.482
  115.3 2.8 reshape.458
  120.3 3.0 reshape.461
  125.5 2.8 reshape.464
  130.5 2.8 reshape.467
  135.5 2.8 reshape.470
  185.4 3.1 reshape.466
  245.0 9.3 %fusion.106 = bf16[16,16,1,1024]{3,1,2,0:T(8,128)(2,1)} fusion(f32[]{:T(128)S(6)} %convert_element_type.307, f32[1024]{0:T(1024)S(1)} %copy-done.14, bf16[18,18,1,64]{3,1,0,2:T(8,128)(2,1)S(1)} %bitcast.290, bf16[18,18,1,1024]{3,1,0,2:T(8,128)(2,1)S(1)} %bitcast.287, f32[1024]{0:T(1024)S(1)} %mul.645, f32[1024]{0:T(1024)S(1)} %mul.648, ...), kind=kLoop, calls=%fused_computation.245 | loop fusion | flops 36175872 | bytes 6983684
  254.4 48.1 %all-reduce.4 = (f32[27,64]{1,0:T(8,128)S(1)}, f32[64]{0:T(128)S(1)}, f32[64,64]{1,0:T(8,128)S(1)}) all-reduce(f32[27,64]{1,0:T(8,128)S(1)} %stack.111, f32[64]{0:T(128)S(1)} %copy-done.54, f32[64,64]{1,0:T(8,128)S(1)} %convolution_bitcast_fusion), channel_id=1, replica_groups=mesh['gx'=16,'gy'=16] {'gx'}, use_global_device_ids=true, to_apply=%region_31.32 | all-reduce | flops 5888 | bytes 47104 | tf_op jit(solution)/shard_map/psum | solution.py:165
  302.5 74.8 %all-reduce.3 = (f32[27,64]{1,0:T(8,128)}, f32[64]{0:T(128)}, f32[64,64]{1,0:T(8,128)}) all-reduce(f32[27,64]{1,0:T(8,128)S(1)} %get-tuple-element.32, f32[64]{0:T(128)S(1)} %get-tuple-element.33, f32[64,64]{1,0:T(8,128)S(1)} %get-tuple-element.34), channel_id=1, replica_groups=mesh['gx'=16,'gy'=16] {'gy'}, use_global_device_ids=true, to_apply=%region_32.33 | all-reduce | flops 5888 | bytes 47104 | tf_op jit(solution)/shard_map/psum | solution.py:164
  (267 shorter events, 160.2 us)
Async XLA Ops:
  0.6 53.5 %copy-start = (bf16[64,64]{1,0:T(8,128)(2,1)S(1)}, bf16[64,64]{1,0:T(8,128)(2,1)}, u32[]{:S(2)}) copy-start(bf16[64,64]{1,0:T(8,128)(2,1)} %param.10) | copy-start | bytes 24580
  4.5 14.6 %collective-permute-start = (bf16[1,16,2,1024]{3,2,1,0:T(2,128)(2,1)S(1)}, bf16[1,16,2,1024]{3,2,1,0:T(2,128)(2,1)S(1)}, u32[]{:S(2)}, u32[]{:S(2)}) collective-permute-start(bf16[1,16,2,1024]{3,2,1,0:T(2,128)(2,1)S(1)} %get-tuple-element.78), channel_id=1, source_target_pairs={{0,16},{16,32},{32,48},{48,64},{64,80},{80,96},{96,112},{112,128},... | collective-permute-start | bytes 196616 | tf_op jit(solution)/shard_map/ppermute | solution.py:17
  6.6 12.6 %collective-permute-start.1 = (bf16[1,16,2,1024]{3,2,1,0:T(2,128)(2,1)S(1)}, bf16[1,16,2,1024]{3,2,1,0:T(2,128)(2,1)S(1)}, u32[]{:S(2)}, u32[]{:S(2)}) collective-permute-start(bf16[1,16,2,1024]{3,2,1,0:T(2,128)(2,1)S(1)} %get-tuple-element.79), channel_id=1, source_target_pairs={{16,0},{32,16},{48,32},{64,48},{80,64},{96,80},{112,96},{128,112},... | collective-permute-start | bytes 196616 | tf_op jit(solution)/shard_map/ppermute | solution.py:19
  15.4 20.4 %copy-start.13 = (f32[1024]{0:T(1024)}, f32[1024]{0:T(1024)S(1)}, u32[]{:S(2)}) copy-start(f32[1024]{0:T(1024)S(1)} %mul.642) | copy-start | bytes 12292
  15.5 20.3 %copy-start.15 = (f32[1024]{0:T(1024)}, f32[1024]{0:T(1024)S(1)}, u32[]{:S(2)}) copy-start(f32[1024]{0:T(1024)S(1)} %mul.714) | copy-start | bytes 12292
  15.6 20.2 %copy-start.17 = (f32[1024]{0:T(1024)}, f32[1024]{0:T(1024)S(1)}, u32[]{:S(2)}) copy-start(f32[1024]{0:T(1024)S(1)} %mul.711) | copy-start | bytes 12292
  15.6 20.2 %copy-start.19 = (f32[1024]{0:T(1024)}, f32[1024]{0:T(1024)S(1)}, u32[]{:S(2)}) copy-start(f32[1024]{0:T(1024)S(1)} %mul.708) | copy-start | bytes 12292
  15.7 20.1 %copy-start.21 = (f32[1024]{0:T(1024)}, f32[1024]{0:T(1024)S(1)}, u32[]{:S(2)}) copy-start(f32[1024]{0:T(1024)S(1)} %mul.705) | copy-start | bytes 12292
  15.8 20.0 %copy-start.23 = (f32[1024]{0:T(1024)}, f32[1024]{0:T(1024)S(1)}, u32[]{:S(2)}) copy-start(f32[1024]{0:T(1024)S(1)} %mul.702) | copy-start | bytes 12292
  15.9 20.0 %copy-start.25 = (f32[1024]{0:T(1024)}, f32[1024]{0:T(1024)S(1)}, u32[]{:S(2)}) copy-start(f32[1024]{0:T(1024)S(1)} %mul.699) | copy-start | bytes 12292
  16.0 19.9 %copy-start.27 = (f32[1024]{0:T(1024)}, f32[1024]{0:T(1024)S(1)}, u32[]{:S(2)}) copy-start(f32[1024]{0:T(1024)S(1)} %mul.696) | copy-start | bytes 12292
  16.0 19.8 %copy-start.29 = (f32[1024]{0:T(1024)}, f32[1024]{0:T(1024)S(1)}, u32[]{:S(2)}) copy-start(f32[1024]{0:T(1024)S(1)} %mul.693) | copy-start | bytes 12292
  16.1 19.8 %copy-start.31 = (f32[1024]{0:T(1024)}, f32[1024]{0:T(1024)S(1)}, u32[]{:S(2)}) copy-start(f32[1024]{0:T(1024)S(1)} %mul.690) | copy-start | bytes 12292
  16.2 19.7 %copy-start.33 = (f32[1024]{0:T(1024)}, f32[1024]{0:T(1024)S(1)}, u32[]{:S(2)}) copy-start(f32[1024]{0:T(1024)S(1)} %mul.687) | copy-start | bytes 12292
  16.3 19.6 %copy-start.35 = (f32[1024]{0:T(1024)}, f32[1024]{0:T(1024)S(1)}, u32[]{:S(2)}) copy-start(f32[1024]{0:T(1024)S(1)} %mul.684) | copy-start | bytes 12292
  16.3 19.6 %copy-start.37 = (f32[1024]{0:T(1024)}, f32[1024]{0:T(1024)S(1)}, u32[]{:S(2)}) copy-start(f32[1024]{0:T(1024)S(1)} %mul.681) | copy-start | bytes 12292
  16.4 19.5 %copy-start.39 = (f32[1024]{0:T(1024)}, f32[1024]{0:T(1024)S(1)}, u32[]{:S(2)}) copy-start(f32[1024]{0:T(1024)S(1)} %mul.678) | copy-start | bytes 12292
  19.4 5.6 %collective-permute-start.2 = (bf16[18,1,2,1024]{3,2,1,0:T(2,128)(2,1)S(1)}, bf16[18,1,2,1024]{3,2,1,0:T(2,128)(2,1)S(1)}, u32[]{:S(2)}, u32[]{:S(2)}) collective-permute-start(bf16[18,1,2,1024]{3,2,1,0:T(2,128)(2,1)S(1)} %get-tuple-element.74), channel_id=1, source_target_pairs={{0,1},{1,2},{2,3},{3,4},{4,5},{5,6},{6,7},{7,8},{8,9},{9,10},{10,1... | collective-permute-start | bytes 221192 | tf_op jit(solution)/shard_map/ppermute | solution.py:17
  22.9 6.2 %collective-permute-start.3 = (bf16[18,1,2,1024]{3,2,1,0:T(2,128)(2,1)S(1)}, bf16[18,1,2,1024]{3,2,1,0:T(2,128)(2,1)S(1)}, u32[]{:S(2)}, u32[]{:S(2)}) collective-permute-start(bf16[18,1,2,1024]{3,2,1,0:T(2,128)(2,1)S(1)} %get-tuple-element.75), channel_id=1, source_target_pairs={{1,0},{2,1},{3,2},{4,3},{5,4},{6,5},{7,6},{8,7},{9,8},{10,9},{11,1... | collective-permute-start | bytes 221192 | tf_op jit(solution)/shard_map/ppermute | solution.py:19
  66.8 8.7 %collective-permute-start.4 = (bf16[1,16,2,1024]{3,2,1,0:T(2,128)(2,1)}, bf16[1,16,2,1024]{3,2,1,0:T(2,128)(2,1)}, u32[]{:S(2)}, u32[]{:S(2)}) collective-permute-start(bf16[1,16,2,1024]{3,2,1,0:T(2,128)(2,1)} %get-tuple-element.76), channel_id=1, source_target_pairs={{0,16},{16,32},{32,48},{48,64},{64,80},{80,96},{96,112},{112,128},... | collective-permute-start | bytes 196616 | tf_op jit(solution)/shard_map/ppermute | solution.py:17
  68.7 7.1 %collective-permute-start.5 = (bf16[1,16,2,1024]{3,2,1,0:T(2,128)(2,1)}, bf16[1,16,2,1024]{3,2,1,0:T(2,128)(2,1)}, u32[]{:S(2)}, u32[]{:S(2)}) collective-permute-start(bf16[1,16,2,1024]{3,2,1,0:T(2,128)(2,1)} %get-tuple-element.77), channel_id=1, source_target_pairs={{16,0},{32,16},{48,32},{64,48},{80,64},{96,80},{112,96},{128,112},... | collective-permute-start | bytes 196616 | tf_op jit(solution)/shard_map/ppermute | solution.py:19
  76.7 9.5 %collective-permute-start.6 = (bf16[18,1,2,1024]{3,2,1,0:T(2,128)(2,1)S(1)}, bf16[18,1,2,1024]{3,2,1,0:T(2,128)(2,1)S(1)}, u32[]{:S(2)}, u32[]{:S(2)}) collective-permute-start(bf16[18,1,2,1024]{3,2,1,0:T(2,128)(2,1)S(1)} %get-tuple-element.72), channel_id=1, source_target_pairs={{0,1},{1,2},{2,3},{3,4},{4,5},{5,6},{6,7},{7,8},{8,9},{9,10},{10,1... | collective-permute-start | bytes 221192 | tf_op jit(solution)/shard_map/ppermute | solution.py:17
  80.2 6.2 %collective-permute-start.7 = (bf16[18,1,2,1024]{3,2,1,0:T(2,128)(2,1)S(1)}, bf16[18,1,2,1024]{3,2,1,0:T(2,128)(2,1)S(1)}, u32[]{:S(2)}, u32[]{:S(2)}) collective-permute-start(bf16[18,1,2,1024]{3,2,1,0:T(2,128)(2,1)S(1)} %get-tuple-element.73), channel_id=1, source_target_pairs={{1,0},{2,1},{3,2},{4,3},{5,4},{6,5},{7,6},{8,7},{9,8},{10,9},{11,1... | collective-permute-start | bytes 221192 | tf_op jit(solution)/shard_map/ppermute | solution.py:19
  244.8 132.5 %copy-start.1 = (bf16[64,64]{1,0:T(8,128)(2,1)S(1)}, bf16[64,64]{1,0:T(8,128)(2,1)}, u32[]{:S(2)}) copy-start(bf16[64,64]{1,0:T(8,128)(2,1)} %param.10) | copy-start | bytes 24580
  (41 other events, 321.9 us)
